TPU v7x, 32 devices: a whole 2x2x4 slice. The times are simulated.
32 devices in a mesh: groups: 2 (over x), query: 8 (over z, y), target: 2 (over core).
Axes of the slice: x: 2, y: 2, z: 4, core: 2. Of those that a mesh axis runs over, the one named last changes fastest.
Arguments:
- query_input: bfloat16 [32, 960, 128], P(('groups', 'query')), parts along dimension 0, may hold values from -18 to 18
- target_input: bfloat16 [64, 960, 128], P(('groups', 'query', 'target')), parts along dimension 0, may hold values from -18 to 18
- conv_weight: bfloat16 [3, 3, 128, 128], replicated, may hold values from -0.1875 to 0.1875
- conv_bias: float32 [128], replicated, may hold values from -3 to 3
Outputs:
- flow: float32 [2, 16, 480], P(None, ('groups', 'query')), parts along dimension 1
There are 2 independent parts, one for each index of `groups`. A program takes and returns all parts, laid end to end along the dimension named above; an argument that names none is the same for every part. Nothing has to cross between parts.
All inputs are finite; a program needn't handle non-finite values.
Results may differ from a plain program's by a relative error of at most 0.0026.
Values may be sent and summed in bfloat16 or wider, within the bound.
A program may use at most 64 MiB of HBM per device.

v0:
```python
import math

import jax
import jax.numpy as jnp
from jax import lax
from jax.sharding import PartitionSpec as P

CELL = 0.0625
FLOOR = -1e30


def passed_along(block, axis, distance):
    devices = range(lax.axis_size(axis))
    route = [(i - distance, i) for i in devices if i - distance in devices]
    return lax.ppermute(block, axis, route)


def shifted(value, axis, steps):
    count = lax.axis_size(axis)
    pairs = [(source, (source + steps) % count) for source in range(count)]
    return lax.ppermute(value, axis, pairs)


def merged(value, axis, join):
    pieces = jax.tree.map(lambda part: lax.all_gather(part, axis), value)
    head = jax.tree.map(lambda part: part[0], pieces)
    tail = jax.tree.map(lambda part: part[1:], pieces)
    total, _ = lax.scan(lambda total, slab: (join(total, slab), None), head, tail)
    return total


def swapped(block, axis, apart):
    count = lax.axis_size(axis)
    route = []
    for low in range(count):
        high = low | 1 << apart
        if high != low and high < count:
            route += [(low, high), (high, low)]
    return lax.ppermute(block, axis, route)


def convolve(frame, upper_rim, conv_weight, conv_bias):
    padded = jnp.concatenate([upper_rim, frame], axis=0)
    padded = jnp.pad(padded, ((0, 0), (1, 0), (0, 0)))
    out_rows = frame.shape[0] // 2
    out_cols = frame.shape[1] // 2
    channels = frame.shape[2]
    summed = jnp.zeros((out_rows * out_cols, conv_weight.shape[3]), jnp.float32)
    for tap_row in range(3):
        for tap_col in range(3):
            window = padded[
                tap_row : tap_row + 2 * out_rows : 2, tap_col : tap_col + 2 * out_cols : 2
            ]
            summed = summed + jnp.dot(
                window.reshape(out_rows * out_cols, channels),
                conv_weight[tap_row, tap_col],
                preferred_element_type=jnp.float32,
            )
    return (summed + conv_bias).astype(jnp.bfloat16)


def starting_state(count):
    return (
        jnp.full((count,), FLOOR, jnp.float32),
        jnp.zeros((count,), jnp.float32),
        jnp.zeros((count,), jnp.float32),
        jnp.zeros((count,), jnp.float32),
    )


def absorb(state_now, key_block, block_rows, queries):
    row_count, row_width, channels = key_block.shape
    key_matrix = key_block.reshape(row_count * row_width, channels)
    scores = jnp.einsum("qc,kc->qk", queries, key_matrix, preferred_element_type=jnp.float32) * (
        1.0 / math.sqrt(channels)
    )
    column_x = (
        lax.broadcasted_iota(jnp.int32, (row_count, row_width), 1).astype(jnp.float32) * CELL
    ).reshape(-1)
    row_y = (
        jnp.broadcast_to(block_rows[:, None], (row_count, row_width)).astype(jnp.float32) * CELL
    ).reshape(-1)
    running_max, weight_sum, sum_x, sum_y = state_now
    new_max = jnp.maximum(running_max, jnp.max(scores, axis=1))
    rescale = jnp.exp(running_max - new_max)
    weights = jnp.exp(scores - new_max[:, None])
    weight_sum = weight_sum * rescale + jnp.sum(weights, axis=1)
    sum_x = sum_x * rescale + jnp.dot(weights, column_x, precision=lax.Precision.HIGHEST)
    sum_y = sum_y * rescale + jnp.dot(weights, row_y, precision=lax.Precision.HIGHEST)
    return (new_max, weight_sum, sum_x, sum_y)


def fold_rows(state_now, shard_piece, global_rows, queries, block_keys):
    row_count = shard_piece.shape[0]
    row_width = shard_piece.shape[1]
    stride = max(1, block_keys // row_width)
    full_blocks = row_count // stride
    leftover = row_count - full_blocks * stride
    state_now = absorb(state_now, shard_piece, global_rows, queries)
    return state_now


def combine_partials(first_part, second_part):
    new_max = jnp.maximum(first_part[0], second_part[0])
    first_scale = jnp.exp(first_part[0] - new_max)
    second_scale = jnp.exp(second_part[0] - new_max)
    return (
        new_max,
        first_part[1] * first_scale + second_part[1] * second_scale,
        first_part[2] * first_scale + second_part[2] * second_scale,
        first_part[3] * first_scale + second_part[3] * second_scale,
    )


def displacement(mean_x, mean_y, positions, query_slot, band_rows, row_width):
    query_x = (positions % row_width).astype(jnp.float32) * CELL
    query_y = (query_slot * band_rows + positions // row_width).astype(jnp.float32) * CELL
    return jnp.stack([mean_x - query_x, mean_y - query_y])


def on_device(query_input, target_input, conv_weight, conv_bias):
    query_rim = passed_along(query_input[-1:], "query", 1)
    target_rim = passed_along(target_input[-1:], ("query", "target"), 1)
    queries = convolve(query_input, query_rim, conv_weight, conv_bias)
    targets = convolve(target_input, target_rim, conv_weight, conv_bias)
    row_width = query_input.shape[1] // 2
    band_rows = query_input.shape[0] // 2
    shard_rows = target_input.shape[0] // 2
    channels = targets.shape[1]
    target_block = targets.reshape(shard_rows, row_width, channels)
    query_slot = lax.axis_index("query")
    core_slot = lax.axis_index("target")
    core_count = lax.axis_size("target")
    query_total = lax.axis_size("query")
    query_count = band_rows * row_width
    block_slot = query_slot % 4
    upward = [queries]
    for step in range(3):
        upward.append(passed_along(upward[-1], "query", 1))
    downward = [queries]
    for step in range(3):
        downward.append(passed_along(downward[-1], "query", -1))
    candidates = jnp.stack(
        [downward[3], downward[2], downward[1], queries, upward[1], upward[2], upward[3]]
    )
    block_queries = jnp.concatenate(
        [
            lax.dynamic_index_in_dim(candidates, block_slot - member + 3, 0, keepdims=False)
            for member in range(4)
        ],
        axis=0,
    )
    local_rows = jnp.arange(shard_rows, dtype=jnp.int32)

    def share_rows(share_query):
        return (share_query * core_count + core_slot) * shard_rows + local_rows

    state_now = fold_rows(
        starting_state(4 * query_count), target_block, share_rows(query_slot), block_queries, 1024
    )
    hops = query_total // 4 - 1

    def hop(counter, carried):
        piece, state_inner = carried
        piece = shifted(piece, "query", 4)
        source = (query_slot - 4 * (counter + 1)) % query_total
        return (piece, fold_rows(state_inner, piece, share_rows(source), block_queries, 1024))

    target_piece, state_now = lax.fori_loop(0, hops, hop, (target_block, state_now))
    state_now = merged(state_now, "target", combine_partials)
    for bit in range(2):
        partner = swapped(state_now, "query", bit)
        state_now = combine_partials(state_now, partner)
    running_max, weight_sum, sum_x, sum_y = [
        lax.dynamic_slice_in_dim(member, block_slot * query_count, query_count, 0)
        for member in state_now
    ]
    positions = jnp.arange(query_count, dtype=jnp.int32)
    flow = displacement(
        sum_x / weight_sum, sum_y / weight_sum, positions, query_slot, band_rows, row_width
    )
    return flow.reshape(2, band_rows, row_width)


def solution(mesh):
    placed = (
        P(("groups", "query"), None, None),
        P(("groups", "query", "target"), None, None),
        P(),
        P(),
    )
    return jax.shard_map(
        on_device,
        mesh=mesh,
        in_specs=placed,
        out_specs=P(None, ("groups", "query"), None),
        check_vma=False,
    )
```

profile of v0, /device:TPU:0, one launch (start us, length us, event | category | flops | bytes accessed | tf_op | source)
XLA Modules:
  0.0 85.0 jit_solution(567079724396638801)
XLA Ops:
  0.0 1.0 %slice.138 = bf16[1,960,128]{2,1,0:T(8,128)(2,1)S(1)} slice(bf16[2,960,128]{2,1,0:T(8,128)(2,1)} %param.4), slice={[1:2], [0:960], [0:128]} | slice | bytes 491520 | tf_op jit(solution)/shard_map/slice | solution.py:122
  1.0 4.9 %collective-permute-start = (bf16[1,960,128]{2,1,0:T(8,128)(2,1)S(1)}, bf16[1,960,128]{2,1,0:T(8,128)(2,1)S(1)}, u32[]{:S(2)}, u32[]{:S(2)}) collective-permute-start(bf16[1,960,128]{2,1,0:T(8,128)(2,1)S(1)} %slice.138), channel_id=1, source_target_pairs={{0,2},{2,4},{4,6},{6,8},{8,10},{10,12},{12,14},{1,3},{3,5},{5,7},{... | collective-permute-start | bytes 737288 | tf_op jit(solution)/shard_map/ppermute | solution.py:15
  5.9 1.0 %slice.157 = bf16[1,960,128]{2,1,0:T(8,128)(2,1)S(1)} slice(bf16[2,960,128]{2,1,0:T(8,128)(2,1)} %param.5), slice={[1:2], [0:960], [0:128]} | slice | bytes 491520 | tf_op jit(solution)/shard_map/slice | solution.py:123
  6.9 1.5 %collective-permute-start.7 = (bf16[1,960,128]{2,1,0:T(8,128)(2,1)S(1)}, bf16[1,960,128]{2,1,0:T(8,128)(2,1)S(1)}, u32[]{:S(2)}, u32[]{:S(2)}) collective-permute-start(bf16[1,960,128]{2,1,0:T(8,128)(2,1)S(1)} %slice.157), channel_id=1, source_target_pairs={{0,1},{1,2},{2,3},{3,4},{4,5},{5,6},{6,7},{7,8},{8,9},{9,10},{10,1... | collective-permute-start | bytes 737288 | tf_op jit(solution)/shard_map/ppermute | solution.py:15
  8.4 3.0 %collective-permute-done = bf16[1,960,128]{2,1,0:T(8,128)(2,1)S(1)} collective-permute-done((bf16[1,960,128]{2,1,0:T(8,128)(2,1)S(1)}, bf16[1,960,128]{2,1,0:T(8,128)(2,1)S(1)}, u32[]{:S(2)}, u32[]{:S(2)}) %collective-permute-start) | collective-permute-done | bytes 245792 | tf_op jit(solution)/shard_map/ppermute | solution.py:15
  11.4 1.2 %fusion.26 = bf16[3,961,128]{2,1,0:T(8,128)(2,1)S(1)} fusion(bf16[2,960,128]{2,1,0:T(8,128)(2,1)} %param.4, bf16[1,960,128]{2,1,0:T(8,128)(2,1)S(1)} %collective-permute-done), kind=kLoop, calls=%fused_computation.47 | loop fusion | flops 2583168 | bytes 1475328 | tf_op jit(solution)/shard_map/concatenate | solution.py:43
  17.9 1.3 %collective-permute-start.1 = (bf16[480,128]{1,0:T(8,128)(2,1)S(1)}, bf16[480,128]{1,0:T(8,128)(2,1)S(1)}, u32[]{:S(2)}, u32[]{:S(2)}) collective-permute-start(bf16[480,128]{1,0:T(8,128)(2,1)S(1)} %fusion.20), channel_id=1, source_target_pairs={{2,0},{4,2},{6,4},{8,6},{10,8},{12,10},{14,12},{3,1},{5,3},{7,5},{... | collective-permute-start | bytes 368648 | tf_op jit(solution)/shard_map/ppermute | solution.py:15
  19.2 5.0 %collective-permute-start.4 = (bf16[480,128]{1,0:T(8,128)(2,1)S(1)}, bf16[480,128]{1,0:T(8,128)(2,1)S(1)}, u32[]{:S(2)}, u32[]{:S(2)}) collective-permute-start(bf16[480,128]{1,0:T(8,128)(2,1)S(1)} %fusion.20), channel_id=1, source_target_pairs={{0,2},{2,4},{4,6},{6,8},{8,10},{10,12},{12,14},{1,3},{3,5},{5,7},{... | collective-permute-start | bytes 368648 | tf_op jit(solution)/shard_map/ppermute | solution.py:15
  29.3 1.3 %collective-permute-start.2 = (bf16[480,128]{1,0:T(8,128)(2,1)S(1)}, bf16[480,128]{1,0:T(8,128)(2,1)S(1)}, u32[]{:S(2)}, u32[]{:S(2)}) collective-permute-start(bf16[480,128]{1,0:T(8,128)(2,1)S(1)} %collective-permute-done.1), channel_id=1, source_target_pairs={{2,0},{4,2},{6,4},{8,6},{10,8},{12,10},{14,12},{3,1},{5,3},{7,5},{... | collective-permute-start | bytes 368648 | tf_op jit(solution)/shard_map/ppermute | solution.py:15
  30.8 5.4 %collective-permute-start.5 = (bf16[480,128]{1,0:T(8,128)(2,1)S(1)}, bf16[480,128]{1,0:T(8,128)(2,1)S(1)}, u32[]{:S(2)}, u32[]{:S(2)}) collective-permute-start(bf16[480,128]{1,0:T(8,128)(2,1)S(1)} %collective-permute-done.4), channel_id=1, source_target_pairs={{0,2},{2,4},{4,6},{6,8},{8,10},{10,12},{12,14},{1,3},{3,5},{5,7},{... | collective-permute-start | bytes 368648 | tf_op jit(solution)/shard_map/ppermute | solution.py:15
  36.3 0.7 collective-permute-done.2
  37.0 1.3 %collective-permute-start.3 = (bf16[480,128]{1,0:T(8,128)(2,1)S(1)}, bf16[480,128]{1,0:T(8,128)(2,1)S(1)}, u32[]{:S(2)}, u32[]{:S(2)}) collective-permute-start(bf16[480,128]{1,0:T(8,128)(2,1)S(1)} %collective-permute-done.2), channel_id=1, source_target_pairs={{2,0},{4,2},{6,4},{8,6},{10,8},{12,10},{14,12},{3,1},{5,3},{7,5},{... | collective-permute-start | bytes 368648 | tf_op jit(solution)/shard_map/ppermute | solution.py:15
  38.5 6.1 %collective-permute-start.8 = (bf16[1,480,128]{2,1,0:T(8,128)(2,1)S(1)}, bf16[1,480,128]{2,1,0:T(8,128)(2,1)S(1)}, u32[]{:S(2)}, u32[]{:S(2)}) collective-permute-start(bf16[1,480,128]{2,1,0:T(8,128)(2,1)S(1)} %bitcast.138), channel_id=1, source_target_pairs={{0,8},{2,10},{4,12},{6,14},{8,0},{10,2},{12,4},{14,6},{1,9},{3,11}... | collective-permute-start | bytes 368648 | tf_op jit(solution)/shard_map/while/body/eval_jaxpr/ppermute | solution.py:21
  44.5 2.2 %collective-permute-start.6 = (bf16[480,128]{1,0:T(8,128)(2,1)S(1)}, bf16[480,128]{1,0:T(8,128)(2,1)S(1)}, u32[]{:S(2)}, u32[]{:S(2)}) collective-permute-start(bf16[480,128]{1,0:T(8,128)(2,1)S(1)} %collective-permute-done.5), channel_id=1, source_target_pairs={{0,2},{2,4},{4,6},{6,8},{8,10},{10,12},{12,14},{1,3},{3,5},{5,7},{... | collective-permute-start | bytes 368648 | tf_op jit(solution)/shard_map/ppermute | solution.py:15
  46.9 2.1 %collective-permute-done.6 = bf16[480,128]{1,0:T(8,128)(2,1)S(1)} collective-permute-done((bf16[480,128]{1,0:T(8,128)(2,1)S(1)}, bf16[480,128]{1,0:T(8,128)(2,1)S(1)}, u32[]{:S(2)}, u32[]{:S(2)}) %collective-permute-start.6) | collective-permute-done | bytes 122912 | tf_op jit(solution)/shard_map/ppermute | solution.py:15
  49.1 0.7 multiply_reduce_fusion.1
  49.8 0.7 multiply_reduce_fusion
  50.5 2.5 %fusion.24 = f32[1920]{0:T(1024)S(1)} fusion(f32[480,1]{0,1:T(1,128)S(1)} %bitcast.139, f32[1920,480]{0,1:T(8,128)S(1)} %get-tuple-element.97, f32[1920]{0:T(1024)S(1)} %get-tuple-element.94), kind=kOutput, calls=%fused_computation.45 | convolution fusion | flops 12902400 | bytes 3703680 | tf_op jit(solution)/shard_map/dot_general | solution.py:88
  53.0 1.2 %fusion.1 = (f32[1920]{0:T(1024)S(1)}, f32[1920]{0:T(1024)S(1)}) fusion(f32[1920,480]{0,1:T(8,128)S(1)} %get-tuple-element.97, f32[1920]{0:T(1024)S(1)} %get-tuple-element.94, f32[1920]{0:T(1024)S(1)} %get-tuple-element.95, f32[1920,480]{0,1:T(8,128)S(1)} %get-tuple-element.99), kind=kLoop, calls=%fused_computation.5 | loop fusion | flops 5525760 | bytes 7403520 | tf_op jit(solution)/shard_map/reduce_sum | solution.py:87
  54.2 2.5 %fusion.22 = f32[1920]{0:T(1024)S(1)} fusion(f32[480,1]{0,1:T(1,128)S(1)} %bitcast.140, f32[1920,480]{0,1:T(8,128)S(1)} %get-tuple-element.99, f32[1920]{0:T(1024)S(1)} %get-tuple-element.95), kind=kOutput, calls=%fused_computation.43 | convolution fusion | flops 12902400 | bytes 3703680 | tf_op jit(solution)/shard_map/while/body/eval_jaxpr/dot_general | solution.py:88
  56.8 2.0 %all-gather.3 = f32[2,1,1920]{2,1,0:T(1,128)S(1)} all-gather(f32[1,1,1920]{2,1,0:T(1,128)S(1)} %get-tuple-element.87), channel_id=1, replica_groups=mesh['groups'=2,'query'=8,'target'=2] {'target'}, dimensions={0}, use_global_device_ids=true | all-gather | bytes 23040 | tf_op jit(solution)/shard_map/all_gather | solution.py:25
  58.9 2.5 %fusion.25 = f32[1920]{0:T(1024)S(1)} fusion(f32[1920,480]{0,1:T(8,128)S(1)} %get-tuple-element.97, f32[1920]{0:T(1024)S(1)} %get-tuple-element.94, f32[]{:T(128)S(6)} %mul.154), kind=kOutput, calls=%fused_computation.46 | convolution fusion | flops 12902400 | bytes 3701764 | tf_op jit(solution)/shard_map/dot_general | solution.py:89
  61.4 2.5 %fusion.23 = f32[1920]{0:T(1024)S(1)} fusion(f32[1920,480]{0,1:T(8,128)S(1)} %get-tuple-element.99, f32[1920]{0:T(1024)S(1)} %get-tuple-element.95, f32[]{:T(128)S(6)} %mul.157), kind=kOutput, calls=%fused_computation.44 | convolution fusion | flops 12902400 | bytes 3701764 | tf_op jit(solution)/shard_map/while/body/eval_jaxpr/dot_general | solution.py:89
  63.9 1.8 %all-gather.2 = f32[2,1,1920]{2,1,0:T(1,128)S(1)} all-gather(f32[1,1,1920]{2,1,0:T(1,128)S(1)} %reshape.188), channel_id=2, replica_groups=mesh['groups'=2,'query'=8,'target'=2] {'target'}, dimensions={0}, use_global_device_ids=true | all-gather | bytes 23040 | tf_op jit(solution)/shard_map/all_gather | solution.py:25
  65.8 3.0 %collective-permute-start.10 = (f32[1920]{0:T(1024)S(1)}, f32[1920]{0:T(1024)S(1)}, u32[]{:S(2)}, u32[]{:S(2)}) collective-permute-start(f32[1920]{0:T(1024)S(1)} %get-tuple-element.63), channel_id=1, source_target_pairs={{0,2},{2,0},{4,6},{6,4},{8,10},{10,8},{12,14},{14,12},{1,3},{3,1},... | collective-permute-start | bytes 23048 | tf_op jit(solution)/shard_map/ppermute | solution.py:39
  68.9 1.8 %all-gather.4 = f32[2,1,1920]{2,1,0:T(1,128)S(1)} all-gather(f32[1,1,1920]{2,1,0:T(1,128)S(1)} %get-tuple-element.86), channel_id=1, replica_groups=mesh['groups'=2,'query'=8,'target'=2] {'target'}, dimensions={0}, use_global_device_ids=true | all-gather | bytes 23040 | tf_op jit(solution)/shard_map/all_gather | solution.py:25
  70.7 1.8 %all-gather.5 = f32[2,1,1920]{2,1,0:T(1,128)S(1)} all-gather(f32[1,1,1920]{2,1,0:T(1,128)S(1)} %reshape.194), channel_id=3, replica_groups=mesh['groups'=2,'query'=8,'target'=2] {'target'}, dimensions={0}, use_global_device_ids=true | all-gather | bytes 23040 | tf_op jit(solution)/shard_map/all_gather | solution.py:25
  72.6 3.9 %collective-permute-start.11 = (f32[1920]{0:T(1024)S(1)}, f32[1920]{0:T(1024)S(1)}, u32[]{:S(2)}, u32[]{:S(2)}) collective-permute-start(f32[1920]{0:T(1024)S(1)} %get-tuple-element.93), channel_id=1, source_target_pairs={{0,4},{4,0},{2,6},{6,2},{8,12},{12,8},{10,14},{14,10},{1,5},{5,1},... | collective-permute-start | bytes 23048 | tf_op jit(solution)/shard_map/ppermute | solution.py:39
  76.6 1.9 %collective-permute-start.15 = (f32[1920]{0:T(1024)S(1)}, f32[1920]{0:T(1024)S(1)}, u32[]{:S(2)}, u32[]{:S(2)}) collective-permute-start(f32[1920]{0:T(1024)S(1)} %get-tuple-element.82), channel_id=1, source_target_pairs={{0,2},{2,0},{4,6},{6,4},{8,10},{10,8},{12,14},{14,12},{1,3},{3,1},... | collective-permute-start | bytes 23048 | tf_op jit(solution)/shard_map/ppermute | solution.py:39
  78.6 1.5 %collective-permute-done.13 = f32[1920]{0:T(1024)S(1)} collective-permute-done((f32[1920]{0:T(1024)S(1)}, f32[1920]{0:T(1024)S(1)}, u32[]{:S(2)}, u32[]{:S(2)}) %collective-permute-start.13) | collective-permute-done | bytes 7712 | tf_op jit(solution)/shard_map/ppermute | solution.py:39
  80.7 1.7 %collective-permute-start.16 = (f32[1920]{0:T(1024)S(1)}, f32[1920]{0:T(1024)S(1)}, u32[]{:S(2)}, u32[]{:S(2)}) collective-permute-start(f32[1920]{0:T(1024)S(1)} %get-tuple-element.80), channel_id=1, source_target_pairs={{0,4},{4,0},{2,6},{6,2},{8,12},{12,8},{10,14},{14,10},{1,5},{5,1},... | collective-permute-start | bytes 23048 | tf_op jit(solution)/shard_map/ppermute | solution.py:39
  82.4 1.6 %collective-permute-done.14 = f32[1920]{0:T(1024)S(1)} collective-permute-done((f32[1920]{0:T(1024)S(1)}, f32[1920]{0:T(1024)S(1)}, u32[]{:S(2)}, u32[]{:S(2)}) %collective-permute-start.14) | collective-permute-done | bytes 7712 | tf_op jit(solution)/shard_map/ppermute | solution.py:39
  (84 shorter events, 12.6 us)
Async XLA Ops:
  0.0 15.9 %copy-start = (bf16[3,3,128,128]{3,2,1,0:T(8,128)(2,1)S(1)}, bf16[3,3,128,128]{3,2,1,0:T(8,128)(2,1)}, u32[]{:S(2)}) copy-start(bf16[3,3,128,128]{3,2,1,0:T(8,128)(2,1)} %param.6) | copy-start | bytes 884740
  1.0 10.4 %collective-permute-start = (bf16[1,960,128]{2,1,0:T(8,128)(2,1)S(1)}, bf16[1,960,128]{2,1,0:T(8,128)(2,1)S(1)}, u32[]{:S(2)}, u32[]{:S(2)}) collective-permute-start(bf16[1,960,128]{2,1,0:T(8,128)(2,1)S(1)} %slice.138), channel_id=1, source_target_pairs={{0,2},{2,4},{4,6},{6,8},{8,10},{10,12},{12,14},{1,3},{3,5},{5,7},{... | collective-permute-start | bytes 737288 | tf_op jit(solution)/shard_map/ppermute | solution.py:15
  6.9 17.3 %collective-permute-start.7 = (bf16[1,960,128]{2,1,0:T(8,128)(2,1)S(1)}, bf16[1,960,128]{2,1,0:T(8,128)(2,1)S(1)}, u32[]{:S(2)}, u32[]{:S(2)}) collective-permute-start(bf16[1,960,128]{2,1,0:T(8,128)(2,1)S(1)} %slice.157), channel_id=1, source_target_pairs={{0,1},{1,2},{2,3},{3,4},{4,5},{5,6},{6,7},{7,8},{8,9},{9,10},{10,1... | collective-permute-start | bytes 737288 | tf_op jit(solution)/shard_map/ppermute | solution.py:15
  12.6 5.1 %copy-start.2 = (f32[128]{0:T(128)S(1)}, f32[128]{0:T(128)}, u32[]{:S(2)}) copy-start(f32[128]{0:T(128)} %param.7) | copy-start | bytes 1540
  13.1 11.2 %copy-start.1 = (bf16[2,960,128]{2,1,0:T(8,128)(2,1)S(1)}, bf16[2,960,128]{2,1,0:T(8,128)(2,1)}, u32[]{:S(2)}) copy-start(bf16[2,960,128]{2,1,0:T(8,128)(2,1)} %param.5) | copy-start | bytes 1474564
  17.9 11.4 %collective-permute-start.1 = (bf16[480,128]{1,0:T(8,128)(2,1)S(1)}, bf16[480,128]{1,0:T(8,128)(2,1)S(1)}, u32[]{:S(2)}, u32[]{:S(2)}) collective-permute-start(bf16[480,128]{1,0:T(8,128)(2,1)S(1)} %fusion.20), channel_id=1, source_target_pairs={{2,0},{4,2},{6,4},{8,6},{10,8},{12,10},{14,12},{3,1},{5,3},{7,5},{... | collective-permute-start | bytes 368648 | tf_op jit(solution)/shard_map/ppermute | solution.py:15
  19.2 11.6 %collective-permute-start.4 = (bf16[480,128]{1,0:T(8,128)(2,1)S(1)}, bf16[480,128]{1,0:T(8,128)(2,1)S(1)}, u32[]{:S(2)}, u32[]{:S(2)}) collective-permute-start(bf16[480,128]{1,0:T(8,128)(2,1)S(1)} %fusion.20), channel_id=1, source_target_pairs={{0,2},{2,4},{4,6},{6,8},{8,10},{10,12},{12,14},{1,3},{3,5},{5,7},{... | collective-permute-start | bytes 368648 | tf_op jit(solution)/shard_map/ppermute | solution.py:15
  29.3 7.7 %collective-permute-start.2 = (bf16[480,128]{1,0:T(8,128)(2,1)S(1)}, bf16[480,128]{1,0:T(8,128)(2,1)S(1)}, u32[]{:S(2)}, u32[]{:S(2)}) collective-permute-start(bf16[480,128]{1,0:T(8,128)(2,1)S(1)} %collective-permute-done.1), channel_id=1, source_target_pairs={{2,0},{4,2},{6,4},{8,6},{10,8},{12,10},{14,12},{3,1},{5,3},{7,5},{... | collective-permute-start | bytes 368648 | tf_op jit(solution)/shard_map/ppermute | solution.py:15
  30.8 13.7 %collective-permute-start.5 = (bf16[480,128]{1,0:T(8,128)(2,1)S(1)}, bf16[480,128]{1,0:T(8,128)(2,1)S(1)}, u32[]{:S(2)}, u32[]{:S(2)}) collective-permute-start(bf16[480,128]{1,0:T(8,128)(2,1)S(1)} %collective-permute-done.4), channel_id=1, source_target_pairs={{0,2},{2,4},{4,6},{6,8},{8,10},{10,12},{12,14},{1,3},{3,5},{5,7},{... | collective-permute-start | bytes 368648 | tf_op jit(solution)/shard_map/ppermute | solution.py:15
  37.0 9.8 %collective-permute-start.3 = (bf16[480,128]{1,0:T(8,128)(2,1)S(1)}, bf16[480,128]{1,0:T(8,128)(2,1)S(1)}, u32[]{:S(2)}, u32[]{:S(2)}) collective-permute-start(bf16[480,128]{1,0:T(8,128)(2,1)S(1)} %collective-permute-done.2), channel_id=1, source_target_pairs={{2,0},{4,2},{6,4},{8,6},{10,8},{12,10},{14,12},{3,1},{5,3},{7,5},{... | collective-permute-start | bytes 368648 | tf_op jit(solution)/shard_map/ppermute | solution.py:15
  38.5 11.3 %collective-permute-start.8 = (bf16[1,480,128]{2,1,0:T(8,128)(2,1)S(1)}, bf16[1,480,128]{2,1,0:T(8,128)(2,1)S(1)}, u32[]{:S(2)}, u32[]{:S(2)}) collective-permute-start(bf16[1,480,128]{2,1,0:T(8,128)(2,1)S(1)} %bitcast.138), channel_id=1, source_target_pairs={{0,8},{2,10},{4,12},{6,14},{8,0},{10,2},{12,4},{14,6},{1,9},{3,11}... | collective-permute-start | bytes 368648 | tf_op jit(solution)/shard_map/while/body/eval_jaxpr/ppermute | solution.py:21
  44.5 4.5 %collective-permute-start.6 = (bf16[480,128]{1,0:T(8,128)(2,1)S(1)}, bf16[480,128]{1,0:T(8,128)(2,1)S(1)}, u32[]{:S(2)}, u32[]{:S(2)}) collective-permute-start(bf16[480,128]{1,0:T(8,128)(2,1)S(1)} %collective-permute-done.5), channel_id=1, source_target_pairs={{0,2},{2,4},{4,6},{6,8},{8,10},{10,12},{12,14},{1,3},{3,5},{5,7},{... | collective-permute-start | bytes 368648 | tf_op jit(solution)/shard_map/ppermute | solution.py:15
  65.8 6.8 %collective-permute-start.10 = (f32[1920]{0:T(1024)S(1)}, f32[1920]{0:T(1024)S(1)}, u32[]{:S(2)}, u32[]{:S(2)}) collective-permute-start(f32[1920]{0:T(1024)S(1)} %get-tuple-element.63), channel_id=1, source_target_pairs={{0,2},{2,0},{4,6},{6,4},{8,10},{10,8},{12,14},{14,12},{1,3},{3,1},... | collective-permute-start | bytes 23048 | tf_op jit(solution)/shard_map/ppermute | solution.py:39
  68.8 3.8 %collective-permute-start.9 = (f32[1920]{0:T(1024)S(1)}, f32[1920]{0:T(1024)S(1)}, u32[]{:S(2)}, u32[]{:S(2)}) collective-permute-start(f32[1920]{0:T(1024)S(1)} %get-tuple-element.64), channel_id=1, source_target_pairs={{0,2},{2,0},{4,6},{6,4},{8,10},{10,8},{12,14},{14,12},{1,3},{3,1},... | collective-permute-start | bytes 23048 | tf_op jit(solution)/shard_map/ppermute | solution.py:39
  72.6 6.0 %collective-permute-start.11 = (f32[1920]{0:T(1024)S(1)}, f32[1920]{0:T(1024)S(1)}, u32[]{:S(2)}, u32[]{:S(2)}) collective-permute-start(f32[1920]{0:T(1024)S(1)} %get-tuple-element.93), channel_id=1, source_target_pairs={{0,4},{4,0},{2,6},{6,2},{8,12},{12,8},{10,14},{14,10},{1,5},{5,1},... | collective-permute-start | bytes 23048 | tf_op jit(solution)/shard_map/ppermute | solution.py:39
  76.5 3.7 %collective-permute-start.13 = (f32[1920]{0:T(1024)S(1)}, f32[1920]{0:T(1024)S(1)}, u32[]{:S(2)}, u32[]{:S(2)}) collective-permute-start(f32[1920]{0:T(1024)S(1)} %get-tuple-element.83), channel_id=1, source_target_pairs={{0,2},{2,0},{4,6},{6,4},{8,10},{10,8},{12,14},{14,12},{1,3},{3,1},... | collective-permute-start | bytes 23048 | tf_op jit(solution)/shard_map/ppermute | solution.py:39
  76.6 3.7 %collective-permute-start.15 = (f32[1920]{0:T(1024)S(1)}, f32[1920]{0:T(1024)S(1)}, u32[]{:S(2)}, u32[]{:S(2)}) collective-permute-start(f32[1920]{0:T(1024)S(1)} %get-tuple-element.82), channel_id=1, source_target_pairs={{0,2},{2,0},{4,6},{6,4},{8,10},{10,8},{12,14},{14,12},{1,3},{3,1},... | collective-permute-start | bytes 23048 | tf_op jit(solution)/shard_map/ppermute | solution.py:39
  78.5 3.8 %collective-permute-start.12 = (f32[1920]{0:T(1024)S(1)}, f32[1920]{0:T(1024)S(1)}, u32[]{:S(2)}, u32[]{:S(2)}) collective-permute-start(f32[1920]{0:T(1024)S(1)} %get-tuple-element.92), channel_id=1, source_target_pairs={{0,4},{4,0},{2,6},{6,2},{8,12},{12,8},{10,14},{14,10},{1,5},{5,1},... | collective-permute-start | bytes 23048 | tf_op jit(solution)/shard_map/ppermute | solution.py:39
  80.3 3.7 %collective-permute-start.14 = (f32[1920]{0:T(1024)S(1)}, f32[1920]{0:T(1024)S(1)}, u32[]{:S(2)}, u32[]{:S(2)}) collective-permute-start(f32[1920]{0:T(1024)S(1)} %get-tuple-element.81), channel_id=1, source_target_pairs={{0,4},{4,0},{2,6},{6,2},{8,12},{12,8},{10,14},{14,10},{1,5},{5,1},... | collective-permute-start | bytes 23048 | tf_op jit(solution)/shard_map/ppermute | solution.py:39
  80.7 3.7 %collective-permute-start.16 = (f32[1920]{0:T(1024)S(1)}, f32[1920]{0:T(1024)S(1)}, u32[]{:S(2)}, u32[]{:S(2)}) collective-permute-start(f32[1920]{0:T(1024)S(1)} %get-tuple-element.80), channel_id=1, source_target_pairs={{0,4},{4,0},{2,6},{6,2},{8,12},{12,8},{10,14},{14,10},{1,5},{5,1},... | collective-permute-start | bytes 23048 | tf_op jit(solution)/shard_map/ppermute | solution.py:39
where the time goes:
time: 85.4 us; the launch traced here: 85 us
  starting transfers between devices  40.1 us (47%)
  matrix products  14.5 us (17%)
  local copies, waits for them, and re-layouts  10 us (12%)
  waiting for transfers between devices  9.34 us (11%)
  blocking collectives  7.48 us (9%)
  other arithmetic  2.93 us (3%)
    ppermute x8, starting transfers between devices, passed_along(): return lax.ppermute(block, axis, route)  22.9 us
    ppermute x8, starting transfers between devices, swapped(): return lax.ppermute(block, axis, route)  11.1 us
    all_gather x4, blocking collectives, merged(): pieces = jax.tree.map(lambda part: lax.all_gather(part, axis), value)  7.48 us
    slice x18, local copies, waits for them, and re-layouts, convolve(): padded[tap_row:tap_row + 2 * out_rows:2, tap_col:tap_col + 2 * out_cols:2]  7.1 us
    ppermute x1, starting transfers between devices, shifted(): return lax.ppermute(value, axis, pairs)  6.06 us
    ppermute x8, waiting for transfers between devices, passed_along(): return lax.ppermute(block, axis, route)  5.79 us
    dot_general x2, matrix products, absorb(): jnp.dot(weights, column_x, precision=lax.Precision.HIGHEST)  5.02 us
    dot_general x2, matrix products, absorb(): jnp.dot(weights, row_y, precision=lax.Precision.HIGHEST)  5.02 us
  transfers between devices with their start and end apart: 17, of which 7 were waited for; matrix products, arithmetic and copies ran while one was open for 16% of the time, Pallas kernels for 0%

commit v1 on v0

v1 whole, which is shorter than its diff:
```python
import functools
import math

import jax
import jax.numpy as jnp
from jax import lax
from jax.experimental import pallas as pl
from jax.experimental.pallas import tpu as pltpu
from jax.sharding import PartitionSpec as P

CELL = 0.0625
MESH = pl.DeviceIdType.MESH
MEMBERS = 4
PAD = 8


def kernel(
    queries_total,
    cores,
    q_hbm,
    t_hbm,
    w_hbm,
    bias_hbm,
    out_ref,
    q_in,
    t_in,
    w_ref,
    bias_ref,
    load,
    spread,
    rim_q_out,
    rim_t_out,
    rim_q_in,
    rim_t_in,
    q_all,
    t_all,
    stats_out,
    stats_in,
    rim_send,
    rim_recv,
    q_send,
    q_recv,
    t_send,
    t_recv,
    s_send,
    s_recv,
):
    n = queries_total
    members = MEMBERS
    cols = n // members
    width = t_in.shape[1] // 2
    half = width // cores
    channels = w_ref.shape[2]
    q = lax.axis_index("query")
    c = lax.axis_index("target")
    other = 1 - c
    member = q // cols
    col = q % cols
    share = q * cores + c

    def target(query, core):
        return {"query": query, "target": core}

    barrier = pltpu.get_barrier_semaphore()
    near = [(True, q, other)]
    near += [(q > 0, q - 1, c), (q < n - 1, q + 1, c)]
    near += [((c == 0) & (q > 0), q - 1, other), ((c == 1) & (q < n - 1), q + 1, other)]
    near += [(member > 0, q - cols, c), (member < members - 1, q + cols, c)]
    near += [(True, member * cols + (col + d) % cols, c) for d in range(1, cols)]
    expected = 0
    for present, query, core in near:
        if present is True:
            pl.semaphore_signal(
                barrier, inc=1, device_id=target(query, core), device_id_type=MESH
            )
            expected = expected + 1
        else:

            @pl.when(present)
            def _(query=query, core=core):
                pl.semaphore_signal(
                    barrier, inc=1, device_id=target(query, core), device_id_type=MESH
                )

            expected = expected + present.astype(jnp.int32)

    loads = [
        pltpu.make_async_copy(source, buffer, load.at[index])
        for index, (source, buffer) in enumerate(
            [
                (q_hbm.at[1], q_in.at[1]),
                (t_hbm.at[1], t_in.at[1]),
                (w_hbm.at[0], w_ref.at[0]),
                (q_hbm.at[0], q_in.at[0]),
                (t_hbm.at[0], t_in.at[0]),
                (w_hbm.at[1], w_ref.at[1]),
                (w_hbm.at[2], w_ref.at[2]),
                (bias_hbm, bias_ref),
            ]
        )
    ]
    for copy in loads:
        copy.start()

    for slot in range(4):
        spread[slot, 0:PAD, :] = jnp.zeros((PAD, spread.shape[2]), jnp.float32)

    def taps(slot, first, count):
        parts = [
            spread[slot, pl.ds(PAD - 1 + tap + 2 * first, count, stride=2), :] for tap in range(3)
        ]
        return jnp.concatenate(parts, axis=1).astype(jnp.bfloat16)

    def dot(a, b):
        return jnp.dot(a, b, preferred_element_type=jnp.float32)

    for copy in loads[:3]:
        copy.wait()
    spread[0, PAD:, :] = q_in[1].astype(jnp.float32)
    spread[1, PAD:, :] = t_in[1].astype(jnp.float32)
    first = pl.multiple_of(c * half, 8)
    q_low = taps(0, first, half)
    t_low = taps(1, 0, width)
    rim_q_out[...] = dot(q_low, w_ref[0]).astype(jnp.bfloat16)
    rim_t_out[...] = dot(t_low, w_ref[0]).astype(jnp.bfloat16)

    for copy in loads[3:]:
        copy.wait()
    spread[2, PAD:, :] = q_in[0].astype(jnp.float32)
    spread[3, PAD:, :] = t_in[0].astype(jnp.float32)
    q_sum = dot(q_low, w_ref[2]) + dot(taps(2, first, half), w_ref[1]) + bias_ref[...]
    t_sum = dot(t_low, w_ref[2]) + dot(taps(3, 0, width), w_ref[1]) + bias_ref[...]

    pl.semaphore_wait(barrier, expected)

    def rim_copies():
        following = share + 1
        return (
            pltpu.make_async_remote_copy(
                src_ref=rim_q_out,
                dst_ref=rim_q_in,
                send_sem=rim_send.at[0],
                recv_sem=rim_recv.at[0],
                device_id=target(q + 1, c),
                device_id_type=MESH,
            ),
            pltpu.make_async_remote_copy(
                src_ref=rim_t_out,
                dst_ref=rim_t_in,
                send_sem=rim_send.at[1],
                recv_sem=rim_recv.at[1],
                device_id=target(following // cores, following % cores),
                device_id_type=MESH,
            ),
        )

    rim_q_copy, rim_t_copy = rim_copies()

    @pl.when(q < n - 1)
    def _():
        rim_q_copy.start()

    @pl.when(share < n * cores - 1)
    def _():
        rim_t_copy.start()

    @pl.when(q > 0)
    def _():
        rim_q_copy.wait_recv()

    @pl.when(q == 0)
    def _():
        rim_q_in[...] = jnp.zeros(rim_q_in.shape, jnp.bfloat16)

    scale = math.log2(math.e) / math.sqrt(channels)
    q_all[member] = ((q_sum + rim_q_in[...].astype(jnp.float32)) * scale).astype(jnp.bfloat16)

    halves = [(0, half // 32 * 16), (half // 32 * 16, half - half // 32 * 16)]

    def q_copy(tile, part, upward):
        place, size = halves[part]
        return pltpu.make_async_remote_copy(
            src_ref=q_all.at[tile, pl.ds(place, size)],
            dst_ref=q_all.at[tile, pl.ds(place, size)],
            send_sem=q_send.at[1 if upward else 0, tile, part],
            recv_sem=q_recv.at[tile, part],
            device_id=target(q + cols if upward else q - cols, c),
            device_id_type=MESH,
        )

    def goes(tile, upward):
        if upward:
            return (tile <= member) & (member < members - 1)
        return (tile >= member) & (member > 0)

    def tile_at(step):
        short = jnp.minimum(member, members - 1 - member)
        apart = (step + 1) // 2
        both = member - apart if step % 2 else member + apart
        rest = jnp.where(
            member < members - 1 - member, member + (step - short), member - (step - short)
        )
        return jnp.where(step <= 2 * short, both, rest)

    def pass_on(tile, part):
        for upward in (False, True):

            @pl.when(goes(tile, upward))
            def _(upward=upward):
                q_copy(tile, part, upward).start()

    def take(step):
        tile = tile_at(step)
        for part in range(2):
            q_copy(tile, part, True).wait_recv()
            pass_on(tile, part)

    for part in range(2):
        pass_on(member, part)

    @pl.when(share > 0)
    def _():
        rim_t_copy.wait_recv()

    @pl.when(share == 0)
    def _():
        rim_t_in[...] = jnp.zeros(rim_t_in.shape, jnp.bfloat16)

    t_all[0] = (t_sum + rim_t_in[...].astype(jnp.float32)).astype(jnp.bfloat16)

    def t_copy(d):
        return pltpu.make_async_remote_copy(
            src_ref=t_all.at[0],
            dst_ref=t_all.at[2 * d],
            send_sem=t_send.at[2 * d],
            recv_sem=t_recv.at[2 * d],
            device_id=target(member * cols + (col + d) % cols, c),
            device_id_type=MESH,
        )

    def t_forward(d):
        return pltpu.make_async_remote_copy(
            src_ref=t_all.at[2 * d],
            dst_ref=t_all.at[2 * d + 1],
            send_sem=t_send.at[2 * d + 1],
            recv_sem=t_recv.at[2 * d + 1],
            device_id=target(q, other),
            device_id_type=MESH,
        )

    for d in range(1, cols):
        t_copy(d).start()
    t_forward(0).start()

    row = lax.broadcasted_iota(jnp.int32, (PAD, width), 0)
    place = lax.broadcasted_iota(jnp.int32, (PAD, width), 1) - width // 2
    values = jnp.where(row == 0, 1, jnp.where(row == 1, place, 0)).astype(jnp.bfloat16)

    def piece(tile, slot):
        scores = lax.dot_general(
            t_all[slot], q_all[tile], (((1,), (1,)), ((), ())), preferred_element_type=jnp.float32
        )
        top = jnp.max(scores, axis=0, keepdims=True)
        weights = jnp.exp2(scores - top).astype(jnp.bfloat16)
        sums = dot(values, weights)
        source = member * cols + (col - slot // 2 + cols) % cols
        core = c if slot % 2 == 0 else other
        height = (source * cores + core).astype(jnp.float32) * CELL
        total = sums[0:1]
        return (top, total, sums[1:2] * CELL, total * height)

    def joined(parts):
        top = functools.reduce(jnp.maximum, [part[0] for part in parts])
        scales = [jnp.exp2(part[0] - top) for part in parts]
        return (top,) + tuple(
            functools.reduce(
                jnp.add, [part[index] * factor for part, factor in zip(parts, scales)]
            )
            for index in range(1, 4)
        )

    def s_copy(tile, step, away):
        return pltpu.make_async_remote_copy(
            src_ref=stats_out.at[step],
            dst_ref=stats_in.at[c, member],
            send_sem=s_send.at[step, away],
            recv_sem=s_recv.at[c, member],
            device_id=target(tile * cols + col, c if away == 0 else other),
            device_id_type=MESH,
        )

    def s_arrival(tile, core):
        return pltpu.make_async_remote_copy(
            src_ref=stats_out.at[0],
            dst_ref=stats_in.at[core, tile],
            send_sem=s_send.at[0, 0],
            recv_sem=s_recv.at[core, tile],
            device_id=target(q, other),
            device_id_type=MESH,
        )

    def finish(step, parts):
        tile = member if step == 0 else tile_at(step)
        state = joined(parts)
        for index in range(4):
            stats_out[step, index : index + 1, 0:half] = state[index]
            if step == 0:
                stats_in[c, member, index : index + 1, 0:half] = state[index]
        for away in range(2):
            if step > 0 or away == 1:
                s_copy(tile, step, away).start()

    parts = [piece(member, 0)]
    t_forward(0).wait_recv()
    parts.append(piece(member, 1))
    take(1)
    take(2)
    for d in range(1, cols):
        t_copy(d).wait_recv()
        t_forward(d).start()
    for d in range(1, cols):
        parts.append(piece(member, 2 * d))
    for d in range(1, cols):
        t_forward(d).wait_recv()
        parts.append(piece(member, 2 * d + 1))
    finish(0, parts)
    for step in range(1, members):
        if step > 2:
            take(step)
        finish(step, [piece(tile_at(step), slot) for slot in range(2 * cols)])

    s_arrival(member, other).wait_recv()
    for step in range(1, members):
        for core in range(cores):
            s_arrival(tile_at(step), core).wait_recv()

    for core in range(cores):
        state = joined(
            [
                tuple(stats_in[core, k, index : index + 1, 0:half] for index in range(4))
                for k in range(members)
            ]
        )
        out_ref[0, :, core * half : (core + 1) * half] = state[2] / state[1]
        out_ref[1, :, core * half : (core + 1) * half] = state[3] / state[1]

    @pl.when(q < n - 1)
    def _():
        rim_q_copy.wait_send()

    @pl.when(share < n * cores - 1)
    def _():
        rim_t_copy.wait_send()

    for step in range(members):
        tile = member if step == 0 else tile_at(step)
        for part in range(2):
            for upward in (False, True):

                @pl.when(goes(tile, upward))
                def _(tile=tile, part=part, upward=upward):
                    q_copy(tile, part, upward).wait_send()

    for d in range(1, cols):
        t_copy(d).wait_send()
    for d in range(cols):
        t_forward(d).wait_send()
    for step in range(members):
        tile = member if step == 0 else tile_at(step)
        for away in range(2):
            if step > 0 or away == 1:
                s_copy(tile, step, away).wait_send()


def on_device(query_input, target_input, conv_weight, conv_bias):
    n = lax.axis_size("query")
    cores = lax.axis_size("target")
    cols = n // MEMBERS
    width = target_input.shape[1] // 2
    half = width // cores
    channels = conv_weight.shape[3]
    depth = conv_weight.shape[2]
    assert query_input.shape[0] == 2 and target_input.shape[0] == 2
    assert cores == 2 and n % MEMBERS == 0
    weight = conv_weight.reshape(3, 3 * depth, channels)
    bf16 = jnp.bfloat16
    means = pl.pallas_call(
        functools.partial(kernel, n, cores),
        out_shape=jax.ShapeDtypeStruct((2, 1, width), jnp.float32),
        in_specs=[pl.BlockSpec(memory_space=pl.ANY)] * 4,
        out_specs=pl.BlockSpec(memory_space=pltpu.VMEM),
        scratch_shapes=[
            pltpu.VMEM((2, 2 * width, depth), bf16),
            pltpu.VMEM((2, 2 * width, depth), bf16),
            pltpu.VMEM((3, 3 * depth, channels), bf16),
            pltpu.VMEM((1, channels), jnp.float32),
            pltpu.SemaphoreType.DMA((8,)),
            pltpu.VMEM((4, PAD + 2 * width, depth), jnp.float32),
            pltpu.VMEM((half, channels), bf16),
            pltpu.VMEM((width, channels), bf16),
            pltpu.VMEM((half, channels), bf16),
            pltpu.VMEM((width, channels), bf16),
            pltpu.VMEM((MEMBERS, half, channels), bf16),
            pltpu.VMEM((2 * cols, width, channels), bf16),
            pltpu.VMEM((MEMBERS, 8, 256), jnp.float32),
            pltpu.VMEM((cores, MEMBERS, 8, 256), jnp.float32),
            pltpu.SemaphoreType.DMA((2,)),
            pltpu.SemaphoreType.DMA((2,)),
            pltpu.SemaphoreType.DMA((2, MEMBERS, 2)),
            pltpu.SemaphoreType.DMA((MEMBERS, 2)),
            pltpu.SemaphoreType.DMA((2 * cols,)),
            pltpu.SemaphoreType.DMA((2 * cols,)),
            pltpu.SemaphoreType.DMA((MEMBERS, 2)),
            pltpu.SemaphoreType.DMA((2, MEMBERS)),
        ],
        compiler_params=pltpu.CompilerParams(collective_id=0, has_side_effects=True),
    )(query_input, target_input, weight, conv_bias.reshape(1, channels))
    column = lax.broadcasted_iota(jnp.int32, (2, 1, width), 2)
    axis = lax.broadcasted_iota(jnp.int32, (2, 1, width), 0)
    shift = jnp.where(axis == 0, column - width // 2, lax.axis_index("query"))
    return means - shift.astype(jnp.float32) * CELL


def solution(mesh):
    placed = (
        P(("groups", "query"), None, None),
        P(("groups", "query", "target"), None, None),
        P(),
        P(),
    )
    return jax.shard_map(
        on_device,
        mesh=mesh,
        in_specs=placed,
        out_specs=P(None, ("groups", "query"), None),
        check_vma=False,
    )
```

time: 85.4 us -> 28.5 us (0.33)
  starting transfers between devices: 40.1 us -> 0 us
  Pallas kernels: 0 us -> 27 us
  matrix products: 14.5 us -> 0 us
  local copies, waits for them, and re-layouts: 10 us -> 0 us
  waiting for transfers between devices: 9.34 us -> 0 us
  blocking collectives: 7.48 us -> 0 us
  other arithmetic: 2.93 us -> 1.37 us
    ppermute x17 -> x0, starting transfers between devices: 40.1 us -> none  [the longest x8 22.9 us: passed_along(): return lax.ppermute(block, axis, route)]
    pallas_call x0 -> x1, Pallas kernels: none -> 27 us  [on_device(): pl.pallas_call(functools.partial(kernel, n, cores), out_shape=jax.ShapeDt...]
    dot_general x24 -> x0, matrix products: 14.5 us -> none  [the longest x2 5.02 us: absorb(): jnp.dot(weights, column_x, precision=lax.Precision.HIGHEST)]
    ppermute x17 -> x0, waiting for transfers between devices: 9.34 us -> none  [the longest x8 5.79 us: passed_along(): return lax.ppermute(block, axis, route)]
    slice x24 -> x0, local copies, waits for them, and re-layouts: 9.23 us -> none  [the longest x18 7.1 us: convolve(): padded[tap_row:tap_row + 2 * out_rows:2, tap_col:tap_col + 2 * out_cols:2]]
    all_gather x4 -> x0, blocking collectives: 7.48 us -> none  [merged(): pieces = jax.tree.map(lambda part: lax.all_gather(part, axis), value)]
    concatenate x2 -> x0, other arithmetic: 1.42 us -> none  [convolve(): padded = jnp.concatenate([upper_rim, frame], axis=0)]
    reduce_sum x1 -> x0, other arithmetic: 1.22 us -> none  [absorb(): weight_sum = weight_sum * rescale + jnp.sum(weights, axis=1)]
  transfers between devices with their start and end apart: 17 -> 0, of which waited for: 7 -> 0; matrix products, arithmetic and copies ran while one was open for 16% -> 0% of each run, Pallas kernels for 0% -> 0%
where the time goes in v1:
time: 28.5 us; the launch traced here: 28.4 us
  Pallas kernels  27 us (95%)
  other arithmetic  1.37 us (5%)
    pallas_call x1, Pallas kernels, on_device(): pl.pallas_call(functools.partial(kernel, n, cores), out_shape=jax.ShapeDt...  27 us
    sub x1, other arithmetic, on_device(): return means - shift.astype(jnp.float32) * CELL  1.36 us

profile of v1, /device:TPU:0, one launch (start us, length us, event | category | flops | bytes accessed | tf_op | source)
XLA Modules:
  0.0 28.4 jit_solution(5355872584373907460)
XLA Ops:
  0.0 27.0 %shard_map.46 = f32[2,1,480]{2,1,0:T(1,128)} custom-call(bf16[2,960,128]{2,1,0:T(8,128)(2,1)} %q_hbm.1, bf16[2,960,128]{2,1,0:T(8,128)(2,1)} %t_hbm.1, bf16[3,384,128]{2,1,0:T(8,128)(2,1)} %bitcast.2, f32[1,128]{1,0:T(1,128)} %bitcast.3), custom_call_target="tpu_custom_call" | custom-call | tf_op jit(solution)/shard_map/pallas_call | solution.py:387
  27.0 1.4 %fusion.2 = f32[2,1,480]{2,1,0:T(1,128)} fusion(f32[2,1,480]{2,1,0:T(1,128)} %shard_map.46, pred[2]{0:T(512)(128)(4,1)S(1)} %iota_compare_fusion, s32[]{:T(128)S(6)} %axis_index.15, s32[480]{0:T(512)S(1)} %iota_add_fusion), kind=kLoop, calls=%fused_computation.3 | loop fusion | flops 3840 | bytes 9606 | tf_op jit(solution)/shard_map/sub | solution.py:421
  (2 shorter events, 0.0 us)

commit v2 on v1

--- a/solution.py
+++ b/solution.py
@@ -40,6 +40,7 @@
     rim_recv,
     q_send,
     q_recv,
+    ready,
     t_send,
     t_recv,
     s_send,
@@ -164,6 +165,25 @@
     def _():
         rim_t_copy.start()
 
+    for turn in range(members - 2):
+
+        @pl.when(member < members - 1)
+        def _(turn=turn):
+            pl.semaphore_signal(
+                ready.at[turn, 0], inc=1, device_id=target(q + cols, c), device_id_type=MESH
+            )
+
+        @pl.when(member > 0)
+        def _(turn=turn):
+            pl.semaphore_signal(
+                ready.at[turn, 1], inc=1, device_id=target(q - cols, c), device_id_type=MESH
+            )
+            pl.semaphore_wait(ready.at[turn, 0], 1)
+
+        @pl.when(member < members - 1)
+        def _(turn=turn):
+            pl.semaphore_wait(ready.at[turn, 1], 1)
+
     @pl.when(q > 0)
     def _():
         rim_q_copy.wait_recv()
@@ -174,24 +194,6 @@
 
     scale = math.log2(math.e) / math.sqrt(channels)
     q_all[member] = ((q_sum + rim_q_in[...].astype(jnp.float32)) * scale).astype(jnp.bfloat16)
-
-    halves = [(0, half // 32 * 16), (half // 32 * 16, half - half // 32 * 16)]
-
-    def q_copy(tile, part, upward):
-        place, size = halves[part]
-        return pltpu.make_async_remote_copy(
-            src_ref=q_all.at[tile, pl.ds(place, size)],
-            dst_ref=q_all.at[tile, pl.ds(place, size)],
-            send_sem=q_send.at[1 if upward else 0, tile, part],
-            recv_sem=q_recv.at[tile, part],
-            device_id=target(q + cols if upward else q - cols, c),
-            device_id_type=MESH,
-        )
-
-    def goes(tile, upward):
-        if upward:
-            return (tile <= member) & (member < members - 1)
-        return (tile >= member) & (member > 0)
 
     def tile_at(step):
         short = jnp.minimum(member, members - 1 - member)
@@ -202,21 +204,28 @@
         )
         return jnp.where(step <= 2 * short, both, rest)
 
-    def pass_on(tile, part):
-        for upward in (False, True):
-
-            @pl.when(goes(tile, upward))
-            def _(upward=upward):
-                q_copy(tile, part, upward).start()
+    def q_copy(step):
+        return pltpu.make_async_remote_copy(
+            src_ref=q_all.at[member],
+            dst_ref=q_all.at[member],
+            send_sem=q_send.at[step],
+            recv_sem=q_recv.at[member],
+            device_id=target(tile_at(step) * cols + col, c),
+            device_id_type=MESH,
+        )
 
     def take(step):
-        tile = tile_at(step)
-        for part in range(2):
-            q_copy(tile, part, True).wait_recv()
-            pass_on(tile, part)
-
-    for part in range(2):
-        pass_on(member, part)
+        pltpu.make_async_remote_copy(
+            src_ref=q_all.at[member],
+            dst_ref=q_all.at[tile_at(step)],
+            send_sem=q_send.at[step],
+            recv_sem=q_recv.at[tile_at(step)],
+            device_id=target(tile_at(step) * cols + col, c),
+            device_id_type=MESH,
+        ).wait_recv()
+
+    for step in range(members - 1, 0, -1):
+        q_copy(step).start()
 
     @pl.when(share > 0)
     def _():
@@ -310,24 +319,27 @@
             if step > 0 or away == 1:
                 s_copy(tile, step, away).start()
 
-    parts = [piece(member, 0)]
+    tiles = [member] + [tile_at(step) for step in range(1, members)]
+    parts = [[piece(member, 0)]] + [[] for _ in range(1, members)]
     t_forward(0).wait_recv()
-    parts.append(piece(member, 1))
+    parts[0].append(piece(member, 1))
     take(1)
-    take(2)
+    parts[1] += [piece(tiles[1], slot) for slot in range(2)]
     for d in range(1, cols):
         t_copy(d).wait_recv()
         t_forward(d).start()
-    for d in range(1, cols):
-        parts.append(piece(member, 2 * d))
+    for step in range(2):
+        parts[step] += [piece(tiles[step], 2 * d) for d in range(1, cols)]
+    take(2)
+    parts[2] += [piece(tiles[2], slot) for slot in range(2 * cols) if slot < 2 or slot % 2 == 0]
     for d in range(1, cols):
         t_forward(d).wait_recv()
-        parts.append(piece(member, 2 * d + 1))
-    finish(0, parts)
-    for step in range(1, members):
-        if step > 2:
-            take(step)
-        finish(step, [piece(tile_at(step), slot) for slot in range(2 * cols)])
+    for step in range(3):
+        parts[step] += [piece(tiles[step], 2 * d + 1) for d in range(1, cols)]
+        finish(step, parts[step])
+    for step in range(3, members):
+        take(step)
+        finish(step, [piece(tiles[step], slot) for slot in range(2 * cols)])
 
     s_arrival(member, other).wait_recv()
     for step in range(1, members):
@@ -352,15 +364,8 @@
     def _():
         rim_t_copy.wait_send()
 
-    for step in range(members):
-        tile = member if step == 0 else tile_at(step)
-        for part in range(2):
-            for upward in (False, True):
-
-                @pl.when(goes(tile, upward))
-                def _(tile=tile, part=part, upward=upward):
-                    q_copy(tile, part, upward).wait_send()
-
+    for step in range(1, members):
+        q_copy(step).wait_send()
     for d in range(1, cols):
         t_copy(d).wait_send()
     for d in range(cols):
@@ -406,8 +411,9 @@
             pltpu.VMEM((cores, MEMBERS, 8, 256), jnp.float32),
             pltpu.SemaphoreType.DMA((2,)),
             pltpu.SemaphoreType.DMA((2,)),
-            pltpu.SemaphoreType.DMA((2, MEMBERS, 2)),
-            pltpu.SemaphoreType.DMA((MEMBERS, 2)),
+            pltpu.SemaphoreType.DMA((MEMBERS,)),
+            pltpu.SemaphoreType.DMA((MEMBERS,)),
+            pltpu.SemaphoreType.REGULAR((MEMBERS - 2, 2)),
             pltpu.SemaphoreType.DMA((2 * cols,)),
             pltpu.SemaphoreType.DMA((2 * cols,)),
             pltpu.SemaphoreType.DMA((MEMBERS, 2)),

time: 28.5 us -> 24.8 us (0.87)
  Pallas kernels: 27 us -> 23.2 us
    pallas_call x1, Pallas kernels: 27 us -> 23.2 us  [on_device(): pl.pallas_call(functools.partial(kernel, n, cores), out_shape=jax.ShapeDt...]
where the time goes in v2:
time: 24.8 us; the launch traced here: 24.6 us
  Pallas kernels  23.2 us (94%)
  other arithmetic  1.37 us (6%)
    pallas_call x1, Pallas kernels, on_device(): pl.pallas_call(functools.partial(kernel, n, cores), out_shape=jax.ShapeDt...  23.2 us
    sub x1, other arithmetic, on_device(): return means - shift.astype(jnp.float32) * CELL  1.36 us

profile of v2, /device:TPU:0, one launch (start us, length us, event | category | flops | bytes accessed | tf_op | source)
XLA Modules:
  0.0 24.6 jit_solution(2793680305471000031)
XLA Ops:
  0.0 23.2 %shard_map.46 = f32[2,1,480]{2,1,0:T(1,128)} custom-call(bf16[2,960,128]{2,1,0:T(8,128)(2,1)} %q_hbm.1, bf16[2,960,128]{2,1,0:T(8,128)(2,1)} %t_hbm.1, bf16[3,384,128]{2,1,0:T(8,128)(2,1)} %bitcast.2, f32[1,128]{1,0:T(1,128)} %bitcast.3), custom_call_target="tpu_custom_call" | custom-call | tf_op jit(solution)/shard_map/pallas_call | solution.py:392
  23.2 1.4 %fusion.2 = f32[2,1,480]{2,1,0:T(1,128)} fusion(f32[2,1,480]{2,1,0:T(1,128)} %shard_map.46, pred[2]{0:T(512)(128)(4,1)S(1)} %iota_compare_fusion, s32[]{:T(128)S(6)} %axis_index.15, s32[480]{0:T(512)S(1)} %iota_add_fusion), kind=kLoop, calls=%fused_computation.3 | loop fusion | flops 3840 | bytes 9606 | tf_op jit(solution)/shard_map/sub | solution.py:427
  (2 shorter events, 0.0 us)

commit v3 on v2

--- a/solution.py
+++ b/solution.py
@@ -165,24 +165,29 @@
     def _():
         rim_t_copy.start()
 
-    for turn in range(members - 2):
-
+    def ready_signal(turn):
         @pl.when(member < members - 1)
-        def _(turn=turn):
+        def _():
             pl.semaphore_signal(
                 ready.at[turn, 0], inc=1, device_id=target(q + cols, c), device_id_type=MESH
             )
 
         @pl.when(member > 0)
-        def _(turn=turn):
+        def _():
             pl.semaphore_signal(
                 ready.at[turn, 1], inc=1, device_id=target(q - cols, c), device_id_type=MESH
             )
+
+    def ready_wait(turn):
+        @pl.when(member > 0)
+        def _():
             pl.semaphore_wait(ready.at[turn, 0], 1)
 
         @pl.when(member < members - 1)
-        def _(turn=turn):
+        def _():
             pl.semaphore_wait(ready.at[turn, 1], 1)
+
+    ready_signal(0)
 
     @pl.when(q > 0)
     def _():
@@ -204,28 +209,38 @@
         )
         return jnp.where(step <= 2 * short, both, rest)
 
-    def q_copy(step):
+    def q_copy(apart, upward):
         return pltpu.make_async_remote_copy(
             src_ref=q_all.at[member],
             dst_ref=q_all.at[member],
-            send_sem=q_send.at[step],
+            send_sem=q_send.at[1 if upward else 0, apart],
             recv_sem=q_recv.at[member],
-            device_id=target(tile_at(step) * cols + col, c),
-            device_id_type=MESH,
-        )
+            device_id=target(q + apart * cols if upward else q - apart * cols, c),
+            device_id_type=MESH,
+        )
+
+    def q_each(apart, act):
+        for upward in (False, True):
+
+            @pl.when(member + apart < members if upward else member >= apart)
+            def _(upward=upward):
+                act(q_copy(apart, upward))
 
     def take(step):
         pltpu.make_async_remote_copy(
             src_ref=q_all.at[member],
             dst_ref=q_all.at[tile_at(step)],
-            send_sem=q_send.at[step],
+            send_sem=q_send.at[0, step],
             recv_sem=q_recv.at[tile_at(step)],
             device_id=target(tile_at(step) * cols + col, c),
             device_id_type=MESH,
         ).wait_recv()
 
-    for step in range(members - 1, 0, -1):
-        q_copy(step).start()
+    q_each(1, lambda copy: copy.start())
+    for apart in range(2, members - 1):
+        ready_wait(apart - 2)
+        ready_signal(apart - 1)
+        q_each(apart, lambda copy: copy.start())
 
     @pl.when(share > 0)
     def _():
@@ -260,6 +275,8 @@
     for d in range(1, cols):
         t_copy(d).start()
     t_forward(0).start()
+    ready_wait(members - 3)
+    q_each(members - 1, lambda copy: copy.start())
 
     row = lax.broadcasted_iota(jnp.int32, (PAD, width), 0)
     place = lax.broadcasted_iota(jnp.int32, (PAD, width), 1) - width // 2
@@ -270,7 +287,7 @@
             t_all[slot], q_all[tile], (((1,), (1,)), ((), ())), preferred_element_type=jnp.float32
         )
         top = jnp.max(scores, axis=0, keepdims=True)
-        weights = jnp.exp2(scores - top).astype(jnp.bfloat16)
+        weights = jnp.exp2((scores - top).astype(jnp.bfloat16))
         sums = dot(values, weights)
         source = member * cols + (col - slot // 2 + cols) % cols
         core = c if slot % 2 == 0 else other
@@ -364,8 +381,8 @@
     def _():
         rim_t_copy.wait_send()
 
-    for step in range(1, members):
-        q_copy(step).wait_send()
+    for apart in range(1, members):
+        q_each(apart, lambda copy: copy.wait_send())
     for d in range(1, cols):
         t_copy(d).wait_send()
     for d in range(cols):
@@ -407,11 +424,11 @@
             pltpu.VMEM((width, channels), bf16),
             pltpu.VMEM((MEMBERS, half, channels), bf16),
             pltpu.VMEM((2 * cols, width, channels), bf16),
-            pltpu.VMEM((MEMBERS, 8, 256), jnp.float32),
-            pltpu.VMEM((cores, MEMBERS, 8, 256), jnp.float32),
+            pltpu.VMEM((MEMBERS, 4, 256), jnp.float32),
+            pltpu.VMEM((cores, MEMBERS, 4, 256), jnp.float32),
             pltpu.SemaphoreType.DMA((2,)),
             pltpu.SemaphoreType.DMA((2,)),
-            pltpu.SemaphoreType.DMA((MEMBERS,)),
+            pltpu.SemaphoreType.DMA((2, MEMBERS)),
             pltpu.SemaphoreType.DMA((MEMBERS,)),
             pltpu.SemaphoreType.REGULAR((MEMBERS - 2, 2)),
             pltpu.SemaphoreType.DMA((2 * cols,)),

time: 24.8 us -> 24.3 us (0.980)
  Pallas kernels: 23.2 us -> 22.7 us
    pallas_call x1, Pallas kernels: 23.2 us -> 22.7 us  [on_device(): pl.pallas_call(functools.partial(kernel, n, cores), out_shape=jax.ShapeDt...]
where the time goes in v3:
time: 24.3 us; the launch traced here: 24.1 us
  Pallas kernels  22.7 us (93%)
  other arithmetic  1.37 us (6%)
    pallas_call x1, Pallas kernels, on_device(): pl.pallas_call(functools.partial(kernel, n, cores), out_shape=jax.ShapeDt...  22.7 us
    sub x1, other arithmetic, on_device(): return means - shift.astype(jnp.float32) * CELL  1.36 us

profile of v3, /device:TPU:0, one launch (start us, length us, event | category | flops | bytes accessed | tf_op | source)
XLA Modules:
  0.0 24.1 jit_solution(7725384234276348637)
XLA Ops:
  0.0 22.7 %shard_map.46 = f32[2,1,480]{2,1,0:T(1,128)} custom-call(bf16[2,960,128]{2,1,0:T(8,128)(2,1)} %q_hbm.1, bf16[2,960,128]{2,1,0:T(8,128)(2,1)} %t_hbm.1, bf16[3,384,128]{2,1,0:T(8,128)(2,1)} %bitcast.2, f32[1,128]{1,0:T(1,128)} %bitcast.3), custom_call_target="tpu_custom_call" | custom-call | tf_op jit(solution)/shard_map/pallas_call | solution.py:409
  22.7 1.4 %fusion.2 = f32[2,1,480]{2,1,0:T(1,128)} fusion(f32[2,1,480]{2,1,0:T(1,128)} %shard_map.46, pred[2]{0:T(512)(128)(4,1)S(1)} %iota_compare_fusion, s32[]{:T(128)S(6)} %axis_index.15, s32[480]{0:T(512)S(1)} %iota_add_fusion), kind=kLoop, calls=%fused_computation.3 | loop fusion | flops 3840 | bytes 9606 | tf_op jit(solution)/shard_map/sub | solution.py:444
  (2 shorter events, 0.0 us)

commit v4 on v3

--- a/solution.py
+++ b/solution.py
@@ -187,7 +187,9 @@
         def _():
             pl.semaphore_wait(ready.at[turn, 1], 1)
 
-    ready_signal(0)
+    for turn in range(members - 2):
+        ready_signal(turn)
+        ready_wait(turn)
 
     @pl.when(q > 0)
     def _():
@@ -236,10 +238,7 @@
             device_id_type=MESH,
         ).wait_recv()
 
-    q_each(1, lambda copy: copy.start())
-    for apart in range(2, members - 1):
-        ready_wait(apart - 2)
-        ready_signal(apart - 1)
+    for apart in range(members - 1, 0, -1):
         q_each(apart, lambda copy: copy.start())
 
     @pl.when(share > 0)
@@ -275,25 +274,34 @@
     for d in range(1, cols):
         t_copy(d).start()
     t_forward(0).start()
-    ready_wait(members - 3)
-    q_each(members - 1, lambda copy: copy.start())
 
     row = lax.broadcasted_iota(jnp.int32, (PAD, width), 0)
     place = lax.broadcasted_iota(jnp.int32, (PAD, width), 1) - width // 2
     values = jnp.where(row == 0, 1, jnp.where(row == 1, place, 0)).astype(jnp.bfloat16)
 
-    def piece(tile, slot):
-        scores = lax.dot_general(
-            t_all[slot], q_all[tile], (((1,), (1,)), ((), ())), preferred_element_type=jnp.float32
-        )
-        top = jnp.max(scores, axis=0, keepdims=True)
-        weights = jnp.exp2((scores - top).astype(jnp.bfloat16))
-        sums = dot(values, weights)
-        source = member * cols + (col - slot // 2 + cols) % cols
-        core = c if slot % 2 == 0 else other
-        height = (source * cores + core).astype(jnp.float32) * CELL
-        total = sums[0:1]
-        return (top, total, sums[1:2] * CELL, total * height)
+    def block(tile, slots):
+        kept = [
+            lax.dot_general(
+                t_all[slot],
+                q_all[tile],
+                (((1,), (1,)), ((), ())),
+                preferred_element_type=jnp.float32,
+            )
+            for slot in slots
+        ]
+        top = functools.reduce(
+            jnp.maximum, [jnp.max(scores, axis=0, keepdims=True) for scores in kept]
+        )
+        total, sum_x, sum_y = 0.0, 0.0, 0.0
+        for slot, scores in zip(slots, kept):
+            sums = dot(values, jnp.exp2((scores - top).astype(jnp.bfloat16)))
+            source = member * cols + (col - slot // 2 + cols) % cols
+            core = c if slot % 2 == 0 else other
+            height = (source * cores + core).astype(jnp.float32) * CELL
+            total = total + sums[0:1]
+            sum_x = sum_x + sums[1:2]
+            sum_y = sum_y + sums[0:1] * height
+        return (top, total, sum_x * CELL, sum_y)
 
     def joined(parts):
         top = functools.reduce(jnp.maximum, [part[0] for part in parts])
@@ -337,26 +345,24 @@
                 s_copy(tile, step, away).start()
 
     tiles = [member] + [tile_at(step) for step in range(1, members)]
-    parts = [[piece(member, 0)]] + [[] for _ in range(1, members)]
+    every = list(range(2 * cols))
+    direct = every[2::2]
+    handed = every[3::2]
     t_forward(0).wait_recv()
-    parts[0].append(piece(member, 1))
-    take(1)
-    parts[1] += [piece(tiles[1], slot) for slot in range(2)]
+    own = [block(member, [0, 1])]
     for d in range(1, cols):
         t_copy(d).wait_recv()
         t_forward(d).start()
-    for step in range(2):
-        parts[step] += [piece(tiles[step], 2 * d) for d in range(1, cols)]
-    take(2)
-    parts[2] += [piece(tiles[2], slot) for slot in range(2 * cols) if slot < 2 or slot % 2 == 0]
+    own.append(block(member, direct))
+    take(1)
+    first_part = [block(tiles[1], [0, 1] + direct)]
     for d in range(1, cols):
         t_forward(d).wait_recv()
-    for step in range(3):
-        parts[step] += [piece(tiles[step], 2 * d + 1) for d in range(1, cols)]
-        finish(step, parts[step])
-    for step in range(3, members):
+    finish(0, own + [block(member, handed)])
+    finish(1, first_part + [block(tiles[1], handed)])
+    for step in range(2, members):
         take(step)
-        finish(step, [piece(tiles[step], slot) for slot in range(2 * cols)])
+        finish(step, [block(tiles[step], every)])
 
     s_arrival(member, other).wait_recv()
     for step in range(1, members):

time: 24.3 us -> 24.1 us (level)
  no operation moved by 1% of the time
where the time goes in v4:
time: 24.1 us; the launch traced here: 23.9 us
  Pallas kernels  22.6 us (94%)
  other arithmetic  1.37 us (6%)
    pallas_call x1, Pallas kernels, on_device(): pl.pallas_call(functools.partial(kernel, n, cores), out_shape=jax.ShapeDt...  22.6 us
    sub x1, other arithmetic, on_device(): return means - shift.astype(jnp.float32) * CELL  1.36 us

profile of v4, /device:TPU:0, one launch (start us, length us, event | category | flops | bytes accessed | tf_op | source)
XLA Modules:
  0.0 23.9 jit_solution(9109029279991785646)
XLA Ops:
  0.0 22.6 %shard_map.46 = f32[2,1,480]{2,1,0:T(1,128)} custom-call(bf16[2,960,128]{2,1,0:T(8,128)(2,1)} %q_hbm.1, bf16[2,960,128]{2,1,0:T(8,128)(2,1)} %t_hbm.1, bf16[3,384,128]{2,1,0:T(8,128)(2,1)} %bitcast.2, f32[1,128]{1,0:T(1,128)} %bitcast.3), custom_call_target="tpu_custom_call" | custom-call | tf_op jit(solution)/shard_map/pallas_call | solution.py:415
  22.6 1.4 %fusion.2 = f32[2,1,480]{2,1,0:T(1,128)} fusion(f32[2,1,480]{2,1,0:T(1,128)} %shard_map.46, pred[2]{0:T(512)(128)(4,1)S(1)} %iota_compare_fusion, s32[]{:T(128)S(6)} %axis_index.15, s32[480]{0:T(512)S(1)} %iota_add_fusion), kind=kLoop, calls=%fused_computation.3 | loop fusion | flops 3840 | bytes 9606 | tf_op jit(solution)/shard_map/sub | solution.py:450
  (2 shorter events, 0.0 us)

commit v5 on v4

--- a/solution.py
+++ b/solution.py
@@ -354,15 +354,16 @@
         t_copy(d).wait_recv()
         t_forward(d).start()
     own.append(block(member, direct))
-    take(1)
-    first_part = [block(tiles[1], [0, 1] + direct)]
+    last = members - 1
+    take(last)
+    first_part = [block(tiles[last], [0, 1] + direct)]
     for d in range(1, cols):
         t_forward(d).wait_recv()
-    finish(0, own + [block(member, handed)])
-    finish(1, first_part + [block(tiles[1], handed)])
-    for step in range(2, members):
+    finish(last, first_part + [block(tiles[last], handed)])
+    for step in range(last - 1, 0, -1):
         take(step)
         finish(step, [block(tiles[step], every)])
+    finish(0, own + [block(member, handed)])
 
     s_arrival(member, other).wait_recv()
     for step in range(1, members):

time: 24.1 us -> 22.7 us (0.942)
  Pallas kernels: 22.6 us -> 21.1 us
    pallas_call x1, Pallas kernels: 22.6 us -> 21.1 us  [on_device(): pl.pallas_call(functools.partial(kernel, n, cores), out_shape=jax.ShapeDt...]
where the time goes in v5:
time: 22.7 us; the launch traced here: 22.5 us
  Pallas kernels  21.1 us (93%)
  other arithmetic  1.37 us (6%)
    pallas_call x1, Pallas kernels, on_device(): pl.pallas_call(functools.partial(kernel, n, cores), out_shape=jax.ShapeDt...  21.1 us
    sub x1, other arithmetic, on_device(): return means - shift.astype(jnp.float32) * CELL  1.36 us

profile of v5, /device:TPU:0, one launch (start us, length us, event | category | flops | bytes accessed | tf_op | source)
XLA Modules:
  0.0 22.5 jit_solution(10825239568445660513)
XLA Ops:
  0.0 21.1 %shard_map.46 = f32[2,1,480]{2,1,0:T(1,128)} custom-call(bf16[2,960,128]{2,1,0:T(8,128)(2,1)} %q_hbm.1, bf16[2,960,128]{2,1,0:T(8,128)(2,1)} %t_hbm.1, bf16[3,384,128]{2,1,0:T(8,128)(2,1)} %bitcast.2, f32[1,128]{1,0:T(1,128)} %bitcast.3), custom_call_target="tpu_custom_call" | custom-call | tf_op jit(solution)/shard_map/pallas_call | solution.py:416
  21.2 1.4 %fusion.2 = f32[2,1,480]{2,1,0:T(1,128)} fusion(f32[2,1,480]{2,1,0:T(1,128)} %shard_map.46, pred[2]{0:T(512)(128)(4,1)S(1)} %iota_compare_fusion, s32[]{:T(128)S(6)} %axis_index.15, s32[480]{0:T(512)S(1)} %iota_add_fusion), kind=kLoop, calls=%fused_computation.3 | loop fusion | flops 3840 | bytes 9606 | tf_op jit(solution)/shard_map/sub | solution.py:451
  (2 shorter events, 0.0 us)
